TPU v7x, 512 devices: a whole 4x8x8 slice. The times are simulated.
512 devices in a mesh: row: 32 (over x, z), col: 16 (over y, core).
Axes of the slice: x: 4, y: 8, z: 8, core: 2. Of those that a mesh axis runs over, the one named last changes fastest.
Arguments:
- window: float32 [16384, 16384], P('row', 'col'), may hold values from -6 to 6
- leaf_vecs: float32 [2, 16384, 128], P(None, ('row', 'col')), may hold values from -0.25 to 0.25
- leaf_t: float32 [2, 4096, 128], P(None, 'row'), may hold values from -0.25 to 0.25
- node_vecs: float32 [2, 4096, 128], P(None, 'row'), may hold values from -0.5 to 0.5
- node_t: float32 [2, 4096, 128], P(None, 'row'), may hold values from -0.25 to 0.25
Outputs:
- updated: float32 [16384, 16384], P('row', 'col')
All inputs are finite; a program needn't handle non-finite values.
Results may differ from a plain program's by a relative error of at most 0.0002.
Values sent between devices are 32-bit elements; how exact they have to be, the bound alone decides.
A program may use at most 64 MiB of HBM per device.

v0:
```python
import jax
import jax.numpy as jnp
from jax import lax
from jax.sharding import PartitionSpec as P


def partner(shard, axis, stride):
    return lax.ppermute(shard, axis, [(i, i ^ 1 << stride) for i in range(lax.axis_size(axis))])


def matmul(left, right):
    return jnp.dot(left, right, precision=lax.Precision.HIGHEST, preferred_element_type=jnp.float32)


def tree_pair(top_a, top_b, vfac, sfac):
    weight = matmul(sfac.T, top_a + matmul(vfac.T, top_b))
    return (top_a - weight, top_b - matmul(vfac, weight))


def local(window, leaf_vecs, leaf_t, node_vecs, node_t):
    width = leaf_t.shape[-1]
    panels = leaf_t.shape[0]
    levels = lax.axis_size("row").bit_length() - 1
    myself = lax.axis_index("row")
    work = window
    all_rows = lax.all_gather(leaf_vecs, "col", axis=1, tiled=True)
    for panel in range(panels):
        vecs = all_rows[panel]
        inner = matmul(leaf_t[panel].T, matmul(vecs.T, work))
        work = work - matmul(vecs, inner)
        top = work[:width]
        vfac = node_vecs[panel]
        sfac = node_t[panel]
        for level in range(levels):
            lower = myself // (1 << level) % 2 == 0
            got, got_v, got_s = partner((top, vfac, sfac), "row", level)
            part_a = jnp.where(lower, top, got)
            part_b = jnp.where(lower, got, top)
            use_v = jnp.where(lower, got_v, vfac)
            use_s = jnp.where(lower, got_s, sfac)
            new_a, new_b = tree_pair(part_a, part_b, use_v, use_s)
            top = jnp.where(lower, new_a, new_b)
        inner = matmul(sfac.T, matmul(vfac.T, top))
        top = jnp.where(myself == 0, top - matmul(vfac, inner), top)
        work = jnp.concatenate([top, work[width:]], axis=0)
    return work


def solution(mesh):
    placed = (
        P("row", "col"),
        P(None, ("row", "col"), None),
        P(None, "row", None),
        P(None, "row", None),
        P(None, "row", None),
    )
    return jax.shard_map(
        local, mesh=mesh, in_specs=placed, out_specs=P("row", "col"), check_vma=False
    )
```

profile of v0, /device:TPU:8, one launch (start us, length us, event | category | flops | bytes accessed | tf_op | source)
XLA Modules:
  0.0 299.1 jit_solution(1070323362962363642)
XLA Ops:
  0.0 21.7 %all_gather.3 = f32[2,512,128]{2,1,0:T(8,128)S(1)} all-gather(f32[2,32,128]{2,1,0:T(8,128)} %param.6), channel_id=1, replica_groups=mesh['row'=32,'col'=16] {'col'}, dimensions={1}, use_global_device_ids=true | all-gather | bytes 557056 | tf_op jit(solution)/shard_map/all_gather | solution.py:26
  21.7 3.0 %fusion.5 = f32[128,1024]{1,0:T(8,128)S(1)} fusion(f32[512,1024]{1,0:T(8,128)} %param.5, f32[2,512,128]{2,1,0:T(8,128)S(1)} %all_gather.3), kind=kOutput, calls=%fused_computation.63 | convolution fusion | flops 805306368 | bytes 2883584 | tf_op jit(solution)/shard_map/dot_general | solution.py:12
  31.0 3.9 %collective-permute-start.2 = (f32[128,128]{1,0:T(8,128)}, f32[128,128]{1,0:T(8,128)S(1)}, u32[]{:S(2)}, u32[]{:S(2)}) collective-permute-start(f32[128,128]{1,0:T(8,128)} %get-tuple-element.8), channel_id=1, source_target_pairs={{0,16},{16,0},{32,48},{48,32},{64,80},{80,64},{96,112},{112,96},{1... | collective-permute-start | bytes 196616 | tf_op jit(solution)/shard_map/ppermute | solution.py:8
  37.5 9.2 %collective-permute-done.2 = f32[128,128]{1,0:T(8,128)S(1)} collective-permute-done((f32[128,128]{1,0:T(8,128)}, f32[128,128]{1,0:T(8,128)S(1)}, u32[]{:S(2)}, u32[]{:S(2)}) %collective-permute-start.2) | collective-permute-done | bytes 65568 | tf_op jit(solution)/shard_map/ppermute | solution.py:8
  49.9 3.0 collective-permute-start.3
  52.9 3.8 %collective-permute-start.5 = (f32[128,128]{1,0:T(8,128)}, f32[128,128]{1,0:T(8,128)S(1)}, u32[]{:S(2)}, u32[]{:S(2)}) collective-permute-start(f32[128,128]{1,0:T(8,128)} %get-tuple-element.8), channel_id=1, source_target_pairs={{0,32},{16,48},{32,0},{48,16},{64,96},{80,112},{96,64},{112,80},{1... | collective-permute-start | bytes 196616 | tf_op jit(solution)/shard_map/ppermute | solution.py:8
  56.7 3.0 collective-permute-start.4
  59.7 21.9 %collective-permute-done.5 = f32[128,128]{1,0:T(8,128)S(1)} collective-permute-done((f32[128,128]{1,0:T(8,128)}, f32[128,128]{1,0:T(8,128)S(1)}, u32[]{:S(2)}, u32[]{:S(2)}) %collective-permute-start.5) | collective-permute-done | bytes 65568 | tf_op jit(solution)/shard_map/ppermute | solution.py:8
  84.2 7.2 %collective-permute-start.6 = (f32[128,1024]{1,0:T(8,128)S(1)}, f32[128,1024]{1,0:T(8,128)S(1)}, u32[]{:S(2)}, u32[]{:S(2)}) collective-permute-start(f32[128,1024]{1,0:T(8,128)S(1)} %subtract_select_fusion.8), channel_id=1, source_target_pairs={{0,64},{16,80},{32,96},{48,112},{64,0},{80,16},{96,32},{112,48},{1... | collective-permute-start | bytes 1572872 | tf_op jit(solution)/shard_map/ppermute | solution.py:8
  94.0 7.2 %collective-permute-start.7 = (f32[128,128]{1,0:T(8,128)}, f32[128,128]{1,0:T(8,128)S(1)}, u32[]{:S(2)}, u32[]{:S(2)}) collective-permute-start(f32[128,128]{1,0:T(8,128)} %get-tuple-element.6), channel_id=1, source_target_pairs={{0,64},{16,80},{32,96},{48,112},{64,0},{80,16},{96,32},{112,48},{1... | collective-permute-start | bytes 196616 | tf_op jit(solution)/shard_map/ppermute | solution.py:8
  101.2 18.9 %collective-permute-done.8 = f32[128,128]{1,0:T(8,128)S(1)} collective-permute-done((f32[128,128]{1,0:T(8,128)}, f32[128,128]{1,0:T(8,128)S(1)}, u32[]{:S(2)}, u32[]{:S(2)}) %collective-permute-start.8) | collective-permute-done | bytes 65568 | tf_op jit(solution)/shard_map/ppermute | solution.py:8
  124.4 3.6 %collective-permute-start.11 = (f32[128,128]{1,0:T(8,128)}, f32[128,128]{1,0:T(8,128)S(1)}, u32[]{:S(2)}, u32[]{:S(2)}) collective-permute-start(f32[128,128]{1,0:T(8,128)} %get-tuple-element.8), channel_id=1, source_target_pairs={{0,128},{16,144},{32,160},{48,176},{64,192},{80,208},{96,224},{112... | collective-permute-start | bytes 196616 | tf_op jit(solution)/shard_map/ppermute | solution.py:8
  130.4 8.6 %collective-permute-done.11 = f32[128,128]{1,0:T(8,128)S(1)} collective-permute-done((f32[128,128]{1,0:T(8,128)}, f32[128,128]{1,0:T(8,128)S(1)}, u32[]{:S(2)}, u32[]{:S(2)}) %collective-permute-start.11) | collective-permute-done | bytes 65568 | tf_op jit(solution)/shard_map/ppermute | solution.py:8
  141.1 3.1 %collective-permute-start.12 = (f32[128,1024]{1,0:T(8,128)S(1)}, f32[128,1024]{1,0:T(8,128)S(1)}, u32[]{:S(2)}, u32[]{:S(2)}) collective-permute-start(f32[128,1024]{1,0:T(8,128)S(1)} %subtract_select_fusion.6), channel_id=1, source_target_pairs={{0,256},{16,272},{32,288},{48,304},{64,320},{80,336},{96,352},{112... | collective-permute-start | bytes 1572872 | tf_op jit(solution)/shard_map/ppermute | solution.py:8
  144.2 4.2 %collective-permute-start.14 = (f32[128,128]{1,0:T(8,128)}, f32[128,128]{1,0:T(8,128)S(1)}, u32[]{:S(2)}, u32[]{:S(2)}) collective-permute-start(f32[128,128]{1,0:T(8,128)} %get-tuple-element.8), channel_id=1, source_target_pairs={{0,256},{16,272},{32,288},{48,304},{64,320},{80,336},{96,352},{112... | collective-permute-start | bytes 196616 | tf_op jit(solution)/shard_map/ppermute | solution.py:8
  148.4 3.1 %collective-permute-start.13 = (f32[128,128]{1,0:T(8,128)}, f32[128,128]{1,0:T(8,128)S(1)}, u32[]{:S(2)}, u32[]{:S(2)}) collective-permute-start(f32[128,128]{1,0:T(8,128)} %get-tuple-element.6), channel_id=1, source_target_pairs={{0,256},{16,272},{32,288},{48,304},{64,320},{80,336},{96,352},{112... | collective-permute-start | bytes 196616 | tf_op jit(solution)/shard_map/ppermute | solution.py:8
  153.1 5.5 %collective-permute-done.14 = f32[128,128]{1,0:T(8,128)S(1)} collective-permute-done((f32[128,128]{1,0:T(8,128)}, f32[128,128]{1,0:T(8,128)S(1)}, u32[]{:S(2)}, u32[]{:S(2)}) %collective-permute-start.14) | collective-permute-done | bytes 65568 | tf_op jit(solution)/shard_map/ppermute | solution.py:8
  162.9 3.4 %fusion = f32[1024,128]{1,0:T(8,128)S(1)} fusion(f32[384,1024]{1,0:T(8,128)S(1)} %slice.50, f32[128,1024]{1,0:T(8,128)S(1)} %fusion.2, f32[2,512,128]{2,1,0:T(8,128)S(1)} %all_gather.3), kind=kOutput, calls=%fused_computation.4 | convolution fusion | flops 805830656 | bytes 2883584 | tf_op jit(solution)/shard_map/dot_general | solution.py:12
  171.0 3.7 %collective-permute-start.17 = (f32[128,128]{1,0:T(8,128)S(1)}, f32[128,128]{1,0:T(8,128)S(1)}, u32[]{:S(2)}, u32[]{:S(2)}) collective-permute-start(f32[128,128]{1,0:T(8,128)S(1)} %copy-done.9), channel_id=1, source_target_pairs={{0,16},{16,0},{32,48},{48,32},{64,80},{80,64},{96,112},{112,96},{1... | collective-permute-start | bytes 196616 | tf_op jit(solution)/shard_map/ppermute | solution.py:8
  176.8 7.2 %collective-permute-done.17 = f32[128,128]{1,0:T(8,128)S(1)} collective-permute-done((f32[128,128]{1,0:T(8,128)S(1)}, f32[128,128]{1,0:T(8,128)S(1)}, u32[]{:S(2)}, u32[]{:S(2)}) %collective-permute-start.17) | collective-permute-done | bytes 65568 | tf_op jit(solution)/shard_map/ppermute | solution.py:8
  186.0 4.9 %collective-permute-start.18 = (f32[128,1024]{1,0:T(8,128)S(1)}, f32[128,1024]{1,0:T(8,128)S(1)}, u32[]{:S(2)}, u32[]{:S(2)}) collective-permute-start(f32[128,1024]{1,0:T(8,128)S(1)} %subtract_select_fusion.4), channel_id=1, source_target_pairs={{0,32},{16,48},{32,0},{48,16},{64,96},{80,112},{96,64},{112,80},{1... | collective-permute-start | bytes 1572872 | tf_op jit(solution)/shard_map/ppermute | solution.py:8
  192.9 4.8 %collective-permute-start.19 = (f32[128,128]{1,0:T(8,128)S(1)}, f32[128,128]{1,0:T(8,128)S(1)}, u32[]{:S(2)}, u32[]{:S(2)}) collective-permute-start(f32[128,128]{1,0:T(8,128)S(1)} %copy-done.8), channel_id=1, source_target_pairs={{0,32},{16,48},{32,0},{48,16},{64,96},{80,112},{96,64},{112,80},{1... | collective-permute-start | bytes 196616 | tf_op jit(solution)/shard_map/ppermute | solution.py:8
  197.7 18.6 %collective-permute-done.20 = f32[128,128]{1,0:T(8,128)S(1)} collective-permute-done((f32[128,128]{1,0:T(8,128)S(1)}, f32[128,128]{1,0:T(8,128)S(1)}, u32[]{:S(2)}, u32[]{:S(2)}) %collective-permute-start.20) | collective-permute-done | bytes 65568 | tf_op jit(solution)/shard_map/ppermute | solution.py:8
  218.3 4.4 %collective-permute-start.21 = (f32[128,1024]{1,0:T(8,128)S(1)}, f32[128,1024]{1,0:T(8,128)S(1)}, u32[]{:S(2)}, u32[]{:S(2)}) collective-permute-start(f32[128,1024]{1,0:T(8,128)S(1)} %subtract_select_fusion.3), channel_id=1, source_target_pairs={{0,64},{16,80},{32,96},{48,112},{64,0},{80,16},{96,32},{112,48},{1... | collective-permute-start | bytes 1572872 | tf_op jit(solution)/shard_map/ppermute | solution.py:8
  222.8 5.3 %collective-permute-start.23 = (f32[128,128]{1,0:T(8,128)S(1)}, f32[128,128]{1,0:T(8,128)S(1)}, u32[]{:S(2)}, u32[]{:S(2)}) collective-permute-start(f32[128,128]{1,0:T(8,128)S(1)} %copy-done.9), channel_id=1, source_target_pairs={{0,64},{16,80},{32,96},{48,112},{64,0},{80,16},{96,32},{112,48},{1... | collective-permute-start | bytes 196616 | tf_op jit(solution)/shard_map/ppermute | solution.py:8
  228.1 4.4 %collective-permute-start.22 = (f32[128,128]{1,0:T(8,128)S(1)}, f32[128,128]{1,0:T(8,128)S(1)}, u32[]{:S(2)}, u32[]{:S(2)}) collective-permute-start(f32[128,128]{1,0:T(8,128)S(1)} %copy-done.8), channel_id=1, source_target_pairs={{0,64},{16,80},{32,96},{48,112},{64,0},{80,16},{96,32},{112,48},{1... | collective-permute-start | bytes 196616 | tf_op jit(solution)/shard_map/ppermute | solution.py:8
  232.5 19.9 %collective-permute-done.23 = f32[128,128]{1,0:T(8,128)S(1)} collective-permute-done((f32[128,128]{1,0:T(8,128)S(1)}, f32[128,128]{1,0:T(8,128)S(1)}, u32[]{:S(2)}, u32[]{:S(2)}) %collective-permute-start.23) | collective-permute-done | bytes 65568 | tf_op jit(solution)/shard_map/ppermute | solution.py:8
  257.1 3.8 %collective-permute-start.26 = (f32[128,128]{1,0:T(8,128)S(1)}, f32[128,128]{1,0:T(8,128)S(1)}, u32[]{:S(2)}, u32[]{:S(2)}) collective-permute-start(f32[128,128]{1,0:T(8,128)S(1)} %copy-done.9), channel_id=1, source_target_pairs={{0,128},{16,144},{32,160},{48,176},{64,192},{80,208},{96,224},{112... | collective-permute-start | bytes 196616 | tf_op jit(solution)/shard_map/ppermute | solution.py:8
  263.0 9.9 %collective-permute-done.26 = f32[128,128]{1,0:T(8,128)S(1)} collective-permute-done((f32[128,128]{1,0:T(8,128)S(1)}, f32[128,128]{1,0:T(8,128)S(1)}, u32[]{:S(2)}, u32[]{:S(2)}) %collective-permute-start.26) | collective-permute-done | bytes 65568 | tf_op jit(solution)/shard_map/ppermute | solution.py:8
  277.8 4.5 %collective-permute-start.29 = (f32[128,128]{1,0:T(8,128)S(1)}, f32[128,128]{1,0:T(8,128)S(1)}, u32[]{:S(2)}, u32[]{:S(2)}) collective-permute-start(f32[128,128]{1,0:T(8,128)S(1)} %copy-done.9), channel_id=1, source_target_pairs={{0,256},{16,272},{32,288},{48,304},{64,320},{80,336},{96,352},{112... | collective-permute-start | bytes 196616 | tf_op jit(solution)/shard_map/ppermute | solution.py:8
  282.3 3.1 %collective-permute-start.28 = (f32[128,128]{1,0:T(8,128)S(1)}, f32[128,128]{1,0:T(8,128)S(1)}, u32[]{:S(2)}, u32[]{:S(2)}) collective-permute-start(f32[128,128]{1,0:T(8,128)S(1)} %copy-done.8), channel_id=1, source_target_pairs={{0,256},{16,272},{32,288},{48,304},{64,320},{80,336},{96,352},{112... | collective-permute-start | bytes 196616 | tf_op jit(solution)/shard_map/ppermute | solution.py:8
  285.4 8.0 %collective-permute-done.29 = f32[128,128]{1,0:T(8,128)S(1)} collective-permute-done((f32[128,128]{1,0:T(8,128)S(1)}, f32[128,128]{1,0:T(8,128)S(1)}, u32[]{:S(2)}, u32[]{:S(2)}) %collective-permute-start.29) | collective-permute-done | bytes 65568 | tf_op jit(solution)/shard_map/ppermute | solution.py:8
  (99 shorter events, 61.4 us)
Async XLA Ops:
  0.0 24.7 %copy-start.6 = (f32[2,128,128]{2,1,0:T(8,128)S(1)}, f32[2,128,128]{2,1,0:T(8,128)}, u32[]{:S(2)}) copy-start(f32[2,128,128]{2,1,0:T(8,128)} %param.7) | copy-start | bytes 393220
  28.4 18.3 %collective-permute-start = (f32[128,1024]{1,0:T(8,128)}, f32[128,1024]{1,0:T(8,128)S(1)}, u32[]{:S(2)}, u32[]{:S(2)}) collective-permute-start(f32[128,1024]{1,0:T(8,128)} %slice.49), channel_id=1, source_target_pairs={{0,16},{16,0},{32,48},{48,32},{64,80},{80,64},{96,112},{112,96},{1... | collective-permute-start | bytes 1572872 | tf_op jit(solution)/shard_map/ppermute | solution.py:8
  31.0 15.7 %collective-permute-start.2 = (f32[128,128]{1,0:T(8,128)}, f32[128,128]{1,0:T(8,128)S(1)}, u32[]{:S(2)}, u32[]{:S(2)}) collective-permute-start(f32[128,128]{1,0:T(8,128)} %get-tuple-element.8), channel_id=1, source_target_pairs={{0,16},{16,0},{32,48},{48,32},{64,80},{80,64},{96,112},{112,96},{1... | collective-permute-start | bytes 196616 | tf_op jit(solution)/shard_map/ppermute | solution.py:8
  35.6 11.9 %collective-permute-start.1 = (f32[128,128]{1,0:T(8,128)}, f32[128,128]{1,0:T(8,128)S(1)}, u32[]{:S(2)}, u32[]{:S(2)}) collective-permute-start(f32[128,128]{1,0:T(8,128)} %get-tuple-element.6), channel_id=1, source_target_pairs={{0,16},{16,0},{32,48},{48,32},{64,80},{80,64},{96,112},{112,96},{1... | collective-permute-start | bytes 196616 | tf_op jit(solution)/shard_map/ppermute | solution.py:8
  49.9 31.7 %collective-permute-start.3 = (f32[128,1024]{1,0:T(8,128)S(1)}, f32[128,1024]{1,0:T(8,128)S(1)}, u32[]{:S(2)}, u32[]{:S(2)}) collective-permute-start(f32[128,1024]{1,0:T(8,128)S(1)} %subtract_select_fusion.9), channel_id=1, source_target_pairs={{0,32},{16,48},{32,0},{48,16},{64,96},{80,112},{96,64},{112,80},{1... | collective-permute-start | bytes 1572872 | tf_op jit(solution)/shard_map/ppermute | solution.py:8
  52.9 28.7 %collective-permute-start.5 = (f32[128,128]{1,0:T(8,128)}, f32[128,128]{1,0:T(8,128)S(1)}, u32[]{:S(2)}, u32[]{:S(2)}) collective-permute-start(f32[128,128]{1,0:T(8,128)} %get-tuple-element.8), channel_id=1, source_target_pairs={{0,32},{16,48},{32,0},{48,16},{64,96},{80,112},{96,64},{112,80},{1... | collective-permute-start | bytes 196616 | tf_op jit(solution)/shard_map/ppermute | solution.py:8
  56.7 26.2 %collective-permute-start.4 = (f32[128,128]{1,0:T(8,128)}, f32[128,128]{1,0:T(8,128)S(1)}, u32[]{:S(2)}, u32[]{:S(2)}) collective-permute-start(f32[128,128]{1,0:T(8,128)} %get-tuple-element.6), channel_id=1, source_target_pairs={{0,32},{16,48},{32,0},{48,16},{64,96},{80,112},{96,64},{112,80},{1... | collective-permute-start | bytes 196616 | tf_op jit(solution)/shard_map/ppermute | solution.py:8
  84.2 35.9 %collective-permute-start.6 = (f32[128,1024]{1,0:T(8,128)S(1)}, f32[128,1024]{1,0:T(8,128)S(1)}, u32[]{:S(2)}, u32[]{:S(2)}) collective-permute-start(f32[128,1024]{1,0:T(8,128)S(1)} %subtract_select_fusion.8), channel_id=1, source_target_pairs={{0,64},{16,80},{32,96},{48,112},{64,0},{80,16},{96,32},{112,48},{1... | collective-permute-start | bytes 1572872 | tf_op jit(solution)/shard_map/ppermute | solution.py:8
  91.4 28.7 %collective-permute-start.8 = (f32[128,128]{1,0:T(8,128)}, f32[128,128]{1,0:T(8,128)S(1)}, u32[]{:S(2)}, u32[]{:S(2)}) collective-permute-start(f32[128,128]{1,0:T(8,128)} %get-tuple-element.8), channel_id=1, source_target_pairs={{0,64},{16,80},{32,96},{48,112},{64,0},{80,16},{96,32},{112,48},{1... | collective-permute-start | bytes 196616 | tf_op jit(solution)/shard_map/ppermute | solution.py:8
  94.0 26.8 %collective-permute-start.7 = (f32[128,128]{1,0:T(8,128)}, f32[128,128]{1,0:T(8,128)S(1)}, u32[]{:S(2)}, u32[]{:S(2)}) collective-permute-start(f32[128,128]{1,0:T(8,128)} %get-tuple-element.6), channel_id=1, source_target_pairs={{0,64},{16,80},{32,96},{48,112},{64,0},{80,16},{96,32},{112,48},{1... | collective-permute-start | bytes 196616 | tf_op jit(solution)/shard_map/ppermute | solution.py:8
  122.1 16.9 %collective-permute-start.9 = (f32[128,1024]{1,0:T(8,128)S(1)}, f32[128,1024]{1,0:T(8,128)S(1)}, u32[]{:S(2)}, u32[]{:S(2)}) collective-permute-start(f32[128,1024]{1,0:T(8,128)S(1)} %subtract_select_fusion.7), channel_id=1, source_target_pairs={{0,128},{16,144},{32,160},{48,176},{64,192},{80,208},{96,224},{112... | collective-permute-start | bytes 1572872 | tf_op jit(solution)/shard_map/ppermute | solution.py:8
  124.4 14.7 %collective-permute-start.11 = (f32[128,128]{1,0:T(8,128)}, f32[128,128]{1,0:T(8,128)S(1)}, u32[]{:S(2)}, u32[]{:S(2)}) collective-permute-start(f32[128,128]{1,0:T(8,128)} %get-tuple-element.8), channel_id=1, source_target_pairs={{0,128},{16,144},{32,160},{48,176},{64,192},{80,208},{96,224},{112... | collective-permute-start | bytes 196616 | tf_op jit(solution)/shard_map/ppermute | solution.py:8
  128.0 11.8 %collective-permute-start.10 = (f32[128,128]{1,0:T(8,128)}, f32[128,128]{1,0:T(8,128)S(1)}, u32[]{:S(2)}, u32[]{:S(2)}) collective-permute-start(f32[128,128]{1,0:T(8,128)} %get-tuple-element.6), channel_id=1, source_target_pairs={{0,128},{16,144},{32,160},{48,176},{64,192},{80,208},{96,224},{112... | collective-permute-start | bytes 196616 | tf_op jit(solution)/shard_map/ppermute | solution.py:8
  141.1 17.6 %collective-permute-start.12 = (f32[128,1024]{1,0:T(8,128)S(1)}, f32[128,1024]{1,0:T(8,128)S(1)}, u32[]{:S(2)}, u32[]{:S(2)}) collective-permute-start(f32[128,1024]{1,0:T(8,128)S(1)} %subtract_select_fusion.6), channel_id=1, source_target_pairs={{0,256},{16,272},{32,288},{48,304},{64,320},{80,336},{96,352},{112... | collective-permute-start | bytes 1572872 | tf_op jit(solution)/shard_map/ppermute | solution.py:8
  144.2 14.4 %collective-permute-start.14 = (f32[128,128]{1,0:T(8,128)}, f32[128,128]{1,0:T(8,128)S(1)}, u32[]{:S(2)}, u32[]{:S(2)}) collective-permute-start(f32[128,128]{1,0:T(8,128)} %get-tuple-element.8), channel_id=1, source_target_pairs={{0,256},{16,272},{32,288},{48,304},{64,320},{80,336},{96,352},{112... | collective-permute-start | bytes 196616 | tf_op jit(solution)/shard_map/ppermute | solution.py:8
  148.4 10.9 %collective-permute-start.13 = (f32[128,128]{1,0:T(8,128)}, f32[128,128]{1,0:T(8,128)S(1)}, u32[]{:S(2)}, u32[]{:S(2)}) collective-permute-start(f32[128,128]{1,0:T(8,128)} %get-tuple-element.6), channel_id=1, source_target_pairs={{0,256},{16,272},{32,288},{48,304},{64,320},{80,336},{96,352},{112... | collective-permute-start | bytes 196616 | tf_op jit(solution)/shard_map/ppermute | solution.py:8
  168.7 116.7 %copy-start.2 = (f32[512,1024]{1,0:T(8,128)}, f32[512,1024]{1,0:T(8,128)S(1)}, u32[]{:S(2)}) copy-start(f32[512,1024]{1,0:T(8,128)S(1)} %bitcast_subtract_fusion) | copy-start | bytes 6291460
  168.8 15.2 %collective-permute-start.15 = (f32[128,1024]{1,0:T(8,128)S(1)}, f32[128,1024]{1,0:T(8,128)S(1)}, u32[]{:S(2)}, u32[]{:S(2)}) collective-permute-start(f32[128,1024]{1,0:T(8,128)S(1)} %slice.52), channel_id=1, source_target_pairs={{0,16},{16,0},{32,48},{48,32},{64,80},{80,64},{96,112},{112,96},{1... | collective-permute-start | bytes 1572872 | tf_op jit(solution)/shard_map/ppermute | solution.py:8
  171.0 13.0 %collective-permute-start.17 = (f32[128,128]{1,0:T(8,128)S(1)}, f32[128,128]{1,0:T(8,128)S(1)}, u32[]{:S(2)}, u32[]{:S(2)}) collective-permute-start(f32[128,128]{1,0:T(8,128)S(1)} %copy-done.9), channel_id=1, source_target_pairs={{0,16},{16,0},{32,48},{48,32},{64,80},{80,64},{96,112},{112,96},{1... | collective-permute-start | bytes 196616 | tf_op jit(solution)/shard_map/ppermute | solution.py:8
  174.7 10.0 %collective-permute-start.16 = (f32[128,128]{1,0:T(8,128)S(1)}, f32[128,128]{1,0:T(8,128)S(1)}, u32[]{:S(2)}, u32[]{:S(2)}) collective-permute-start(f32[128,128]{1,0:T(8,128)S(1)} %copy-done.8), channel_id=1, source_target_pairs={{0,16},{16,0},{32,48},{48,32},{64,80},{80,64},{96,112},{112,96},{1... | collective-permute-start | bytes 196616 | tf_op jit(solution)/shard_map/ppermute | solution.py:8
  186.0 30.2 %collective-permute-start.18 = (f32[128,1024]{1,0:T(8,128)S(1)}, f32[128,1024]{1,0:T(8,128)S(1)}, u32[]{:S(2)}, u32[]{:S(2)}) collective-permute-start(f32[128,1024]{1,0:T(8,128)S(1)} %subtract_select_fusion.4), channel_id=1, source_target_pairs={{0,32},{16,48},{32,0},{48,16},{64,96},{80,112},{96,64},{112,80},{1... | collective-permute-start | bytes 1572872 | tf_op jit(solution)/shard_map/ppermute | solution.py:8
  191.0 25.3 %collective-permute-start.20 = (f32[128,128]{1,0:T(8,128)S(1)}, f32[128,128]{1,0:T(8,128)S(1)}, u32[]{:S(2)}, u32[]{:S(2)}) collective-permute-start(f32[128,128]{1,0:T(8,128)S(1)} %copy-done.9), channel_id=1, source_target_pairs={{0,32},{16,48},{32,0},{48,16},{64,96},{80,112},{96,64},{112,80},{1... | collective-permute-start | bytes 196616 | tf_op jit(solution)/shard_map/ppermute | solution.py:8
  192.9 24.1 %collective-permute-start.19 = (f32[128,128]{1,0:T(8,128)S(1)}, f32[128,128]{1,0:T(8,128)S(1)}, u32[]{:S(2)}, u32[]{:S(2)}) collective-permute-start(f32[128,128]{1,0:T(8,128)S(1)} %copy-done.8), channel_id=1, source_target_pairs={{0,32},{16,48},{32,0},{48,16},{64,96},{80,112},{96,64},{112,80},{1... | collective-permute-start | bytes 196616 | tf_op jit(solution)/shard_map/ppermute | solution.py:8
  218.3 34.1 %collective-permute-start.21 = (f32[128,1024]{1,0:T(8,128)S(1)}, f32[128,1024]{1,0:T(8,128)S(1)}, u32[]{:S(2)}, u32[]{:S(2)}) collective-permute-start(f32[128,1024]{1,0:T(8,128)S(1)} %subtract_select_fusion.3), channel_id=1, source_target_pairs={{0,64},{16,80},{32,96},{48,112},{64,0},{80,16},{96,32},{112,48},{1... | collective-permute-start | bytes 1572872 | tf_op jit(solution)/shard_map/ppermute | solution.py:8
  222.8 29.7 %collective-permute-start.23 = (f32[128,128]{1,0:T(8,128)S(1)}, f32[128,128]{1,0:T(8,128)S(1)}, u32[]{:S(2)}, u32[]{:S(2)}) collective-permute-start(f32[128,128]{1,0:T(8,128)S(1)} %copy-done.9), channel_id=1, source_target_pairs={{0,64},{16,80},{32,96},{48,112},{64,0},{80,16},{96,32},{112,48},{1... | collective-permute-start | bytes 196616 | tf_op jit(solution)/shard_map/ppermute | solution.py:8
  228.1 25.7 %collective-permute-start.22 = (f32[128,128]{1,0:T(8,128)S(1)}, f32[128,128]{1,0:T(8,128)S(1)}, u32[]{:S(2)}, u32[]{:S(2)}) collective-permute-start(f32[128,128]{1,0:T(8,128)S(1)} %copy-done.8), channel_id=1, source_target_pairs={{0,64},{16,80},{32,96},{48,112},{64,0},{80,16},{96,32},{112,48},{1... | collective-permute-start | bytes 196616 | tf_op jit(solution)/shard_map/ppermute | solution.py:8
  255.1 17.8 %collective-permute-start.24 = (f32[128,1024]{1,0:T(8,128)S(1)}, f32[128,1024]{1,0:T(8,128)S(1)}, u32[]{:S(2)}, u32[]{:S(2)}) collective-permute-start(f32[128,1024]{1,0:T(8,128)S(1)} %subtract_select_fusion.2), channel_id=1, source_target_pairs={{0,128},{16,144},{32,160},{48,176},{64,192},{80,208},{96,224},{112... | collective-permute-start | bytes 1572872 | tf_op jit(solution)/shard_map/ppermute | solution.py:8
  257.1 15.8 %collective-permute-start.26 = (f32[128,128]{1,0:T(8,128)S(1)}, f32[128,128]{1,0:T(8,128)S(1)}, u32[]{:S(2)}, u32[]{:S(2)}) collective-permute-start(f32[128,128]{1,0:T(8,128)S(1)} %copy-done.9), channel_id=1, source_target_pairs={{0,128},{16,144},{32,160},{48,176},{64,192},{80,208},{96,224},{112... | collective-permute-start | bytes 196616 | tf_op jit(solution)/shard_map/ppermute | solution.py:8
  260.9 12.7 %collective-permute-start.25 = (f32[128,128]{1,0:T(8,128)S(1)}, f32[128,128]{1,0:T(8,128)S(1)}, u32[]{:S(2)}, u32[]{:S(2)}) collective-permute-start(f32[128,128]{1,0:T(8,128)S(1)} %copy-done.8), channel_id=1, source_target_pairs={{0,128},{16,144},{32,160},{48,176},{64,192},{80,208},{96,224},{112... | collective-permute-start | bytes 196616 | tf_op jit(solution)/shard_map/ppermute | solution.py:8
  274.9 18.5 %collective-permute-start.27 = (f32[128,1024]{1,0:T(8,128)S(1)}, f32[128,1024]{1,0:T(8,128)S(1)}, u32[]{:S(2)}, u32[]{:S(2)}) collective-permute-start(f32[128,1024]{1,0:T(8,128)S(1)} %subtract_select_fusion.1), channel_id=1, source_target_pairs={{0,256},{16,272},{32,288},{48,304},{64,320},{80,336},{96,352},{112... | collective-permute-start | bytes 1572872 | tf_op jit(solution)/shard_map/ppermute | solution.py:8
  277.8 15.6 %collective-permute-start.29 = (f32[128,128]{1,0:T(8,128)S(1)}, f32[128,128]{1,0:T(8,128)S(1)}, u32[]{:S(2)}, u32[]{:S(2)}) collective-permute-start(f32[128,128]{1,0:T(8,128)S(1)} %copy-done.9), channel_id=1, source_target_pairs={{0,256},{16,272},{32,288},{48,304},{64,320},{80,336},{96,352},{112... | collective-permute-start | bytes 196616 | tf_op jit(solution)/shard_map/ppermute | solution.py:8
  282.3 11.8 %collective-permute-start.28 = (f32[128,128]{1,0:T(8,128)S(1)}, f32[128,128]{1,0:T(8,128)S(1)}, u32[]{:S(2)}, u32[]{:S(2)}) collective-permute-start(f32[128,128]{1,0:T(8,128)S(1)} %copy-done.8), channel_id=1, source_target_pairs={{0,256},{16,272},{32,288},{48,304},{64,320},{80,336},{96,352},{112... | collective-permute-start | bytes 196616 | tf_op jit(solution)/shard_map/ppermute | solution.py:8
  (9 other events, 57.4 us)
where the time goes:
time: 300 us; the launch traced here: 299 us
  waiting for transfers between devices  129 us (43%)
  starting transfers between devices  105 us (35%)
  matrix products  36.6 us (12%)
  blocking collectives  21.7 us (7%)
  local copies, waits for them, and re-layouts  3.79 us (1%)
    ppermute x30, waiting for transfers between devices, partner(): lax.ppermute(shard, axis, [(i, i ^ 1 << stride) for i in range(lax.axis_s...  129 us
    ppermute x30, starting transfers between devices, partner(): lax.ppermute(shard, axis, [(i, i ^ 1 << stride) for i in range(lax.axis_s...  105 us
    dot_general x42, matrix products, matmul(): jnp.dot(left, right, precision=lax.Precision.HIGHEST, preferred_element_t...  36.6 us
    all_gather x1, blocking collectives, local(): all_rows = lax.all_gather(leaf_vecs, 'col', axis=1, tiled=True)  21.7 us
  transfers between devices with their start and end apart: 30, of which 13 were waited for; matrix products, arithmetic and copies ran while one was open for 3% of the time, Pallas kernels for 0%

commit v1 on v0

v1 whole, which is shorter than its diff:
```python
import functools

import jax
import jax.numpy as jnp
from jax import lax
from jax.experimental import pallas as pl
from jax.experimental.pallas import tpu as pltpu
from jax.sharding import PartitionSpec as P

MESH = pl.DeviceIdType.MESH
F32, BF16 = jnp.float32, jnp.bfloat16
NB = 128
NX = 4
CORES = 2
CHUNKS = 2


def split(value):
    high = value.astype(BF16)
    return high, (value - high.astype(F32)).astype(BF16)


def dot(left, right):
    return jnp.dot(left, right, preferred_element_type=F32)


def dot_nt(left, right):
    return lax.dot_general(left, right, (((1,), (1,)), ((), ())), preferred_element_type=F32)


def wide(value):
    high, low = split(value)
    return jnp.concatenate([high, high, low], axis=1)


def tall(value):
    high, low = split(value)
    return jnp.concatenate([high, high, low], axis=0)


def mixed(value, axis):
    high, low = split(value)
    return jnp.concatenate([high, low, high], axis=axis)


def kernel(sizes, *refs):
    nx, nz, ny, nc, mr, ncl, npan = sizes
    (window, leaf_vecs, leaf_t, node_vecs, node_t, out,
     work, yvec, lfac, vsz, vsx, stay, tz, tx, back, part, inn,
     yk, yt, lk, zv1, zs1, zvn, xv1, xs1, xvn,
     loc, barrier_free, ys, yr, ps, pr, hs, hr, zs, zr, xs, xr, ls, lr, osem) = refs
    del barrier_free
    cw = ncl // nc
    zc = cw // nz
    zx = zc // nx
    tw = min(256, cw)
    tiles = cw // tw
    me_r, me_c = lax.axis_index("row"), lax.axis_index("col")
    x, z = me_r // nz, lax.rem(me_r, nz)
    y, core = me_c // CORES, lax.rem(me_c, CORES)
    other = 1 - core

    def wait(sem, ref):
        pltpu.make_async_copy(ref, ref, sem).wait()

    def near(src, dst, sem):
        pltpu.make_async_copy(src, dst, sem).start()

    def far(src, dst, ssem, rsem, row, col):
        pltpu.make_async_remote_copy(
            src_ref=src, dst_ref=dst, send_sem=ssem, recv_sem=rsem,
            device_id={"row": row, "col": col}, device_id_type=MESH,
        ).start()

    def order(n):
        steps = []
        for d in range(n // 2, 0, -1):
            steps.append(d)
            if n - d != d:
                steps.append(n - d)
        return steps

    near(window, work, loc.at[0])
    for p in range(npan):
        near(leaf_vecs.at[p], yvec.at[p, y, core], loc.at[1])
        near(node_vecs.at[p, me_c], vsz.at[p, y, core, z, 0], loc.at[2])
        near(node_t.at[p, me_c], vsz.at[p, y, core, z, 1], loc.at[2])
        near(node_vecs.at[p, me_c], vsx.at[p, y, core, x, 0], loc.at[4])
        near(node_t.at[p, me_c], vsx.at[p, y, core, x, 1], loc.at[4])
    near(leaf_t, lfac, loc.at[3])

    barrier = pltpu.get_barrier_semaphore()
    for dx in range(nx):
        for dz in range(nz):
            if dx or dz:
                row = lax.rem(x + dx, nx) * nz + lax.rem(z + dz, nz)
                pl.semaphore_signal(barrier, inc=1, device_id={"row": row, "col": me_c}, device_id_type=MESH)
    for dy in range(1, ny):
        col = lax.rem(y + dy, ny) * CORES + core
        pl.semaphore_signal(barrier, inc=1, device_id={"row": me_r, "col": col}, device_id_type=MESH)
    pl.semaphore_signal(barrier, inc=1, device_id={"row": me_r, "col": y * CORES + other}, device_id_type=MESH)
    wait(loc.at[1], yvec.at[pl.ds(0, npan), 0, 0])
    wait(loc.at[2], vsz.at[pl.ds(0, npan), 0, 0, 0])
    wait(loc.at[4], vsx.at[pl.ds(0, npan), 0, 0, 0])
    pl.semaphore_wait(barrier, nx * nz - 1 + ny - 1 + 1)

    def send_y(p):
        for dy in order(ny):
            far(yvec.at[p, y, core], yvec.at[p, y, core], ys.at[p], yr.at[p], me_r, lax.rem(y + dy, ny) * CORES + core)

    def sibling(ref, ssem, rsem):
        far(ref, ref, ssem, rsem, me_r, y * CORES + other)

    def take_y(p):
        if ny > 1:
            wait(yr.at[p], yvec.at[p, pl.ds(0, ny - 1), 0])
        sibling(yvec.at[p, :, core], ps.at[0, p], pr.at[0, p])

    def send_first(p):
        for dz in order(nz):
            far(vsz.at[p, y, core, z], vsz.at[p, y, core, z], hs.at[0, 0, p], hr.at[0, 0, p],
                x * nz + lax.rem(z + dz, nz), me_c)
        for dx in order(nx):
            far(vsx.at[p, y, core, x], vsx.at[p, y, core, x], hs.at[0, 1, p], hr.at[0, 1, p],
                lax.rem(x + dx, nx) * nz + z, me_c)

    def send_second(k, p):
        buf, n = ((vsz, nz), (vsx, nx))[k]
        wait(hr.at[0, k, p], buf.at[p, 0, 0, pl.ds(0, n - 1)])
        for dy in order(ny):
            far(buf.at[p, y, core], buf.at[p, y, core], hs.at[1, k, p], hr.at[1, k, p],
                me_r, lax.rem(y + dy, ny) * CORES + core)

    def send_third(k, p):
        buf = (vsz, vsx)[k]
        if ny > 1:
            wait(hr.at[1, k, p], buf.at[p, pl.ds(0, ny - 1), 0])
        sibling(buf.at[p, :, core], ps.at[1 + k, p], pr.at[1 + k, p])

    send_y(0)
    for p in range(npan):
        if p:
            send_y(p)
        send_first(p)
    send_second(0, 0)
    take_y(0)
    send_second(1, 0)

    def prep_leaf(p):
        wait(pr.at[0, p], yvec.at[p, :, 0])
        vecs = yvec[p].reshape(mr, NB)
        yk[p] = mixed(vecs, 1)
        high, low = split(vecs.T)
        yt[p, :NB] = high
        yt[p, NB:] = low
        lk[p] = mixed(lfac[p].T, 1)

    wait(loc.at[3], lfac)
    prep_leaf(0)
    wait(loc.at[0], work)

    def reduce_rows(p, value, first, count):
        high, low = split(value)
        both = dot(yt[p, :, first:first + count], high)
        return both[:NB] + both[NB:] + dot(yt[p, :NB, first:first + count], low)

    def column(c, t):
        return pl.ds(pl.multiple_of(c * cw + t * tw, tw), tw)

    def leaf_top(p, c):
        @pl.loop(0, tiles)
        def _(t):
            cols = column(c, t)
            if p == 0:
                top = work[:NB, cols]
                inner = reduce_rows(p, work[:, cols], 0, mr)
            else:
                held = back.at[p - 1, c, pl.ds(t * (tw // zc), tw // zc)]
                top = held[...].reshape(tw, NB).T
                inner = part[:, cols] + reduce_rows(p, top, 0, NB)
            high, low = split(dot(lk[p], tall(inner)))
            stack = jnp.concatenate([high, high, low], axis=0)
            inn[:, cols] = stack
            top = top - dot(yk[p, :NB], stack)
            stay[p, c, pl.ds(t * (tw // zc), tw // zc)] = top.T.reshape(tw // zc, zc, NB)

    def send_z(p, c):
        near(stay.at[p, c, z], tz.at[p, c, z], zr.at[p, c])
        for dz in order(nz):
            zp = lax.rem(z + dz, nz)
            far(stay.at[p, c, zp], tz.at[p, c, z], zs.at[p, c], zr.at[p, c], x * nz + zp, me_c)

    def leaf_rest(p, c):
        @pl.loop(0, tiles)
        def _(t):
            cols = column(c, t)
            rest = work[NB:, cols] - dot(yk[p, NB:], inn[:, cols])
            work[NB:, cols] = rest

    def next_part(p, c):
        @pl.loop(0, tiles)
        def _(t):
            cols = column(c, t)
            part[:, cols] = reduce_rows(p, work[NB:, cols], NB, mr - NB)

    def prep_pairs(k, p):
        buf, n = ((vsz, nz), (vsx, nx))[k]
        v1, s1, vn = ((zv1, zs1, zvn), (xv1, xs1, xvn))[k]
        wait(pr.at[1 + k, p], buf.at[p, :, 0])

        @pl.loop(0, n)
        def _(b):
            vfac = buf[p, :, :, b, 0].reshape(NB, NB)
            high, low = split(vfac)
            v1[b] = jnp.concatenate([high, low, high], axis=0)
            vn[b] = jnp.concatenate([high, low, high], axis=1)
            s1[b] = mixed(buf[p, :, :, b, 1].reshape(NB, NB), 0)

    def pair(buf, rows, a, b, v1, s1, vn):
        top_a = buf[a].reshape(rows, NB)
        top_b = buf[b].reshape(rows, NB)
        weight = dot(wide(top_a + dot(wide(top_b), v1[b])), s1[b])
        return top_a - weight, top_b - dot_nt(wide(weight), vn[b])

    def level(buf, rows, n, bit, v1, s1, vn):
        shape = buf.shape[1:]
        for a in range(n):
            if a >> bit & 1 == 0:
                b = a | 1 << bit
                new_a, new_b = pair(buf, rows, a, b, v1, s1, vn)
                buf[a] = new_a.reshape(shape)
                buf[b] = new_b.reshape(shape)

    def z_stage(p, c):
        wait(zr.at[p, c], tz.at[p, c])
        for bit in range(nz.bit_length() - 1):
            level(tz.at[p, c], zc, nz, bit, zv1, zs1, zvn)

    def send_x(p, c):
        for dx in range(nx):
            xp = lax.rem(x + dx, nx)
            rows = pl.ds(pl.multiple_of(xp * zx, zx), zx)
            for dz in ([0] if dx == 0 else []) + order(nz) + ([0] if dx else []):
                zp = lax.rem(z + dz, nz)
                src, dst = tz.at[p, c, zp, rows], tx.at[p, c, x, z]
                if dx == 0 and dz == 0:
                    near(src, dst, xr.at[p, c])
                else:
                    far(src, dst, xs.at[p, c], xr.at[p, c], xp * nz + zp, me_c)

    def x_stage(p, c):
        wait(xr.at[p, c], tx.at[p, c])
        rows = nz * zx
        for bit in range(nx.bit_length() - 1):
            level(tx.at[p, c], rows, nx, bit, xv1, xs1, xvn)

        @pl.when(z == 0)
        def _():
            root = tx[p, c, 0].reshape(rows, NB)
            inner = dot(wide(dot(wide(root), xv1[0])), xs1[0])
            tx[p, c, 0] = (root - dot_nt(wide(inner), xvn[0])).reshape(nz, zx, NB)

    def send_l(p, c):
        near(tx.at[p, c, x], back.at[p, c, :, x], lr.at[p, c])
        for dx in order(nx):
            xp = lax.rem(x + dx, nx)
            far(tx.at[p, c, xp], back.at[p, c, :, x], ls.at[p, c], lr.at[p, c], xp * nz + z, me_c)

    def out_rest(c):
        cols = pl.ds(pl.multiple_of(c * cw, cw), cw)
        near(work.at[pl.ds(NB, mr - NB), cols], out.at[pl.ds(NB, mr - NB), cols], osem)

    for p in range(npan):
        @pl.loop(0, nc)
        def _(c):
            if p:
                wait(lr.at[p - 1, c], back.at[p - 1, c])
            leaf_top(p, c)
            send_z(p, c)

        if p == 0:
            send_third(0, 0)
            send_third(1, 0)
            for q in range(1, npan):
                take_y(q)
                send_second(0, q)
                send_second(1, q)
        prep_pairs(0, p)

        @pl.loop(0, nc)
        def _(c):
            leaf_rest(p, c)
            if p == npan - 1:
                out_rest(c)

        @pl.loop(0, nc)
        def _(c):
            z_stage(p, c)
            send_x(p, c)

        prep_pairs(1, p)
        if p + 1 < npan:
            prep_leaf(p + 1)
            send_third(0, p + 1)
            send_third(1, p + 1)

            @pl.loop(0, nc)
            def _(c):
                next_part(p + 1, c)

        @pl.loop(0, nc)
        def _(c):
            x_stage(p, c)
            send_l(p, c)

    last = npan - 1

    @pl.loop(0, nc)
    def _(c):
        wait(lr.at[last, c], back.at[last, c])

        @pl.loop(0, tiles)
        def _(t):
            cols = column(c, t)
            held = back.at[last, c, pl.ds(t * (tw // zc), tw // zc)]
            work[:NB, cols] = held[...].reshape(tw, NB).T
        cols = pl.ds(pl.multiple_of(c * cw, cw), cw)
        near(work.at[pl.ds(0, NB), cols], out.at[pl.ds(0, NB), cols], osem)

    wait(osem, work)
    for p in range(npan):
        if ny > 1:
            wait(ys.at[p], yvec.at[p, pl.ds(0, ny - 1), 0])
            for k, buf in ((0, vsz), (1, vsx)):
                wait(hs.at[1, k, p], buf.at[p, pl.ds(0, ny - 1), 0])
        wait(ps.at[0, p], yvec.at[p, :, 0])
        for k, (buf, n) in enumerate(((vsz, nz), (vsx, nx))):
            wait(hs.at[0, k, p], buf.at[p, 0, 0, pl.ds(0, n - 1)])
            wait(ps.at[1 + k, p], buf.at[p, :, 0])

        @pl.loop(0, nc)
        def _(c):
            wait(zs.at[p, c], stay.at[p, c, pl.ds(0, nz - 1)])
            wait(xs.at[p, c], tx.at[p, c, pl.ds(0, nx - 1)])
            wait(xs.at[p, c], tx.at[p, c, 0, pl.ds(0, nz - 1)])
            wait(ls.at[p, c], tx.at[p, c, pl.ds(0, nx - 1)])


def local(nx, nc, window, leaf_vecs, leaf_t, node_vecs, node_t):
    mr, ncl = window.shape
    npan = leaf_t.shape[0]
    nz = lax.axis_size("row") // nx
    nq = lax.axis_size("col")
    ny = nq // CORES
    vr = NB // nq
    cw = ncl // nc
    zc = cw // nz
    zx = zc // nx
    any_space = pl.BlockSpec(memory_space=pl.ANY)
    dma = pltpu.SemaphoreType.DMA
    scratch = [
        pltpu.VMEM((mr, ncl), F32),
        pltpu.VMEM((npan, ny, CORES, mr // nq, NB), F32),
        pltpu.VMEM((npan, NB, NB), F32),
        pltpu.VMEM((npan, ny, CORES, nz, 2, vr, NB), F32),
        pltpu.VMEM((npan, ny, CORES, nx, 2, vr, NB), F32),
        pltpu.VMEM((npan, nc, nz, zc, NB), F32),
        pltpu.VMEM((npan, nc, nz, zc, NB), F32),
        pltpu.VMEM((npan, nc, nx, nz, zx, NB), F32),
        pltpu.VMEM((npan, nc, nz, nx, zx, NB), F32),
        pltpu.VMEM((NB, ncl), F32),
        pltpu.VMEM((3 * NB, ncl), BF16),
        pltpu.VMEM((npan, mr, 3 * NB), BF16),
        pltpu.VMEM((npan, 2 * NB, mr), BF16),
        pltpu.VMEM((npan, NB, 3 * NB), BF16),
    ]
    for n in (nz, nx):
        scratch += [
            pltpu.VMEM((n, 3 * NB, NB), BF16),
            pltpu.VMEM((n, 3 * NB, NB), BF16),
            pltpu.VMEM((n, NB, 3 * NB), BF16),
        ]
    scratch += [
        dma((5,)), dma((1,)), dma((npan,)), dma((npan,)), dma((3, npan)), dma((3, npan)),
        dma((2, 2, npan)), dma((2, 2, npan)),
        dma((npan, nc)), dma((npan, nc)), dma((npan, nc)), dma((npan, nc)), dma((npan, nc)), dma((npan, nc)),
        dma,
    ]
    return pl.pallas_call(
        functools.partial(kernel, (nx, nz, ny, nc, mr, ncl, npan)),
        out_shape=jax.ShapeDtypeStruct(window.shape, window.dtype),
        in_specs=[any_space] * 5,
        out_specs=any_space,
        scratch_shapes=scratch,
        compiler_params=pltpu.CompilerParams(
            collective_id=0, has_side_effects=True, vmem_limit_bytes=48 * 1024 * 1024
        ),
    )(
        window, leaf_vecs, leaf_t,
        node_vecs.reshape(npan, nq, vr, NB), node_t.reshape(npan, nq, vr, NB),
    )


def build(mesh, nx, nc):
    placed = (
        P("row", "col"),
        P(None, ("row", "col"), None),
        P(None, "row", None),
        P(None, "row", None),
        P(None, "row", None),
    )
    return jax.shard_map(
        functools.partial(local, nx, nc), mesh=mesh, in_specs=placed, out_specs=P("row", "col"), check_vma=False
    )


def solution(mesh):
    return build(mesh, NX, CHUNKS)
```

time: 300 us -> 108 us (0.36)
  the two profiles are of different devices: /device:TPU:8 before, /device:TPU:16 now
where the time goes in v1:
time: 108 us; the launch traced here: 107 us
  Pallas kernels  101 us (94%)
  local copies, waits for them, and re-layouts  6.38 us (6%)
    pallas_call x1, Pallas kernels, local(): pl.pallas_call(functools.partial(kernel, (nx, nz, ny, nc, mr, ncl, npan))...  101 us
    unnamed x11, local copies, waits for them, and re-layouts  6.38 us

profile of v1, /device:TPU:16, one launch (start us, length us, event | category | flops | bytes accessed | tf_op | source)
XLA Modules:
  0.0 107.3 jit_solution(10648771759167543315)
XLA Ops:
  0.0 0.0 copy-start
  0.0 1.6 %copy-done = f32[512,1024]{1,0:T(8,128)S(1)} copy-done((f32[512,1024]{1,0:T(8,128)S(1)}, f32[512,1024]{1,0:T(8,128)}, u32[]{:S(2)}) %copy-start) | copy-done | bytes 2097176
  1.6 0.0 copy-start.1
  1.6 0.9 copy-done.1
  2.5 0.0 copy-start.2
  2.5 0.9 copy-done.2
  3.4 0.0 copy-start.3
  3.4 0.9 copy-done.3
  4.3 0.0 copy-start.4
  4.3 0.8 copy-done.4
  5.1 101.0 %shard_map.55 = f32[512,1024]{1,0:T(8,128)S(1)} custom-call(f32[512,1024]{1,0:T(8,128)S(1)} %copy-done, f32[2,32,128]{2,1,0:T(8,128)S(1)} %copy-done.4, f32[2,128,128]{2,1,0:T(8,128)S(1)} %copy-done.1, f32[2,16,8,128]{3,2,1,0:T(8,128)S(1)} %bitcast.2, f32[2,16,8,128]{3,2,1,0:T(8,128)S(1)} %bitcast.3), custom_call_target="tpu_custom_call" | custom-call | tf_op jit(solution)/shard_map/pallas_call | solution.py:389
  106.0 1.3 %copy.7 = f32[512,1024]{1,0:T(8,128)} copy(f32[512,1024]{1,0:T(8,128)S(1)} %shard_map.55) | data formatting | bytes 4194304
Async XLA Ops:
  0.0 1.6 %copy-start = (f32[512,1024]{1,0:T(8,128)S(1)}, f32[512,1024]{1,0:T(8,128)}, u32[]{:S(2)}) copy-start(f32[512,1024]{1,0:T(8,128)} %refs_0_.1) | copy-start | bytes 6291460
  1.6 0.9 copy-start.1
  2.5 0.9 copy-start.2
  3.4 0.9 copy-start.3
  4.3 0.8 copy-start.4

commit v2 on v1

--- a/solution.py
+++ b/solution.py
@@ -12,7 +12,7 @@
 NB = 128
 NX = 4
 CORES = 2
-CHUNKS = 2
+CHUNKS = 4
 
 
 def split(value):
@@ -104,17 +104,39 @@
     wait(loc.at[4], vsx.at[pl.ds(0, npan), 0, 0, 0])
     pl.semaphore_wait(barrier, nx * nz - 1 + ny - 1 + 1)
 
-    def send_y(p):
-        for dy in order(ny):
-            far(yvec.at[p, y, core], yvec.at[p, y, core], ys.at[p], yr.at[p], me_r, lax.rem(y + dy, ny) * CORES + core)
-
-    def sibling(ref, ssem, rsem):
-        far(ref, ref, ssem, rsem, me_r, y * CORES + other)
-
-    def take_y(p):
-        if ny > 1:
-            wait(yr.at[p], yvec.at[p, pl.ds(0, ny - 1), 0])
-        sibling(yvec.at[p, :, core], ps.at[0, p], pr.at[0, p])
+    turn = 1 - 2 * core
+    rings = (yvec, vsz, vsx)
+
+    def place(shift):
+        return lax.rem(y + turn * shift + 2 * ny, ny)
+
+    ahead, behind = ny // 2, (ny - 1) // 2
+
+    def ring_wait(kind, p, step):
+        if step < ahead:
+            wait(yr.at[kind, p, step], rings[kind].at[p, 0, core])
+        if step < behind:
+            wait(yr.at[kind, p, ahead + step], rings[kind].at[p, 0, core])
+
+    def ring_step(kind, p, step):
+        if step:
+            ring_wait(kind, p, step - 1)
+        if step < ahead:
+            piece = rings[kind].at[p, place(-step), core]
+            far(piece, piece, ys.at[kind, p, step], yr.at[kind, p, step], me_r, place(1) * CORES + core)
+        if step < behind:
+            piece = rings[kind].at[p, place(step), core]
+            far(piece, piece, ys.at[kind, p, ahead + step], yr.at[kind, p, ahead + step],
+                me_r, place(-1) * CORES + core)
+
+    def ring_end(kind, p):
+        ring_wait(kind, p, ahead - 1)
+        ref = rings[kind].at[p, :, core]
+        far(ref, ref, ps.at[kind, p], pr.at[kind, p], me_r, y * CORES + other)
+
+    def first_wait(k, p):
+        buf, n = ((vsz, nz), (vsx, nx))[k]
+        wait(hr.at[0, k, p], buf.at[p, 0, 0, pl.ds(0, n - 1)])
 
     def send_first(p):
         for dz in order(nz):
@@ -124,27 +146,19 @@
             far(vsx.at[p, y, core, x], vsx.at[p, y, core, x], hs.at[0, 1, p], hr.at[0, 1, p],
                 lax.rem(x + dx, nx) * nz + z, me_c)
 
-    def send_second(k, p):
-        buf, n = ((vsz, nz), (vsx, nx))[k]
-        wait(hr.at[0, k, p], buf.at[p, 0, 0, pl.ds(0, n - 1)])
-        for dy in order(ny):
-            far(buf.at[p, y, core], buf.at[p, y, core], hs.at[1, k, p], hr.at[1, k, p],
-                me_r, lax.rem(y + dy, ny) * CORES + core)
-
-    def send_third(k, p):
-        buf = (vsz, vsx)[k]
-        if ny > 1:
-            wait(hr.at[1, k, p], buf.at[p, pl.ds(0, ny - 1), 0])
-        sibling(buf.at[p, :, core], ps.at[1 + k, p], pr.at[1 + k, p])
-
-    send_y(0)
     for p in range(npan):
-        if p:
-            send_y(p)
         send_first(p)
-    send_second(0, 0)
-    take_y(0)
-    send_second(1, 0)
+    ring_step(0, 0, 0)
+    ring_step(0, 0, 1)
+    first_wait(0, 0)
+    ring_step(1, 0, 0)
+    ring_step(0, 0, 2)
+    ring_step(1, 0, 1)
+    ring_step(0, 0, 3)
+    first_wait(1, 0)
+    ring_end(0, 0)
+    ring_step(1, 0, 2)
+    ring_step(2, 0, 0)
 
     def prep_leaf(p):
         wait(pr.at[0, p], yvec.at[p, :, 0])
@@ -279,13 +293,10 @@
             send_z(p, c)
 
         if p == 0:
-            send_third(0, 0)
-            send_third(1, 0)
-            for q in range(1, npan):
-                take_y(q)
-                send_second(0, q)
-                send_second(1, q)
-        prep_pairs(0, p)
+            ring_step(1, 0, 3)
+            ring_step(2, 0, 1)
+        else:
+            ring_end(2, p)
 
         @pl.loop(0, nc)
         def _(c):
@@ -293,16 +304,34 @@
             if p == npan - 1:
                 out_rest(c)
 
+        if p == 0:
+            ring_end(1, 0)
+            ring_step(2, 0, 2)
+            ring_step(2, 0, 3)
+            for q in range(1, npan):
+                first_wait(0, q)
+                first_wait(1, q)
+        prep_pairs(0, p)
+        if p == 0:
+            ring_end(2, 0)
+
         @pl.loop(0, nc)
         def _(c):
             z_stage(p, c)
             send_x(p, c)
-
+            if p + 1 < npan:
+                for step in range(ahead):
+                    @pl.when(c == step)
+                    def _():
+                        ring_step(0, p + 1, step)
+                        ring_step(1, p + 1, step)
+
+        if p + 1 < npan:
+            ring_end(0, p + 1)
+            ring_end(1, p + 1)
         prep_pairs(1, p)
         if p + 1 < npan:
             prep_leaf(p + 1)
-            send_third(0, p + 1)
-            send_third(1, p + 1)
 
             @pl.loop(0, nc)
             def _(c):
@@ -312,6 +341,11 @@
         def _(c):
             x_stage(p, c)
             send_l(p, c)
+            if p + 1 < npan:
+                for step in range(ahead):
+                    @pl.when(c == step)
+                    def _():
+                        ring_step(2, p + 1, step)
 
     last = npan - 1
 
@@ -329,10 +363,9 @@
 
     wait(osem, work)
     for p in range(npan):
-        if ny > 1:
-            wait(ys.at[p], yvec.at[p, pl.ds(0, ny - 1), 0])
-            for k, buf in ((0, vsz), (1, vsx)):
-                wait(hs.at[1, k, p], buf.at[p, pl.ds(0, ny - 1), 0])
+        for kind in range(3):
+            for step in range(ny - 1):
+                wait(ys.at[kind, p, step], rings[kind].at[p, 0, core])
         wait(ps.at[0, p], yvec.at[p, :, 0])
         for k, (buf, n) in enumerate(((vsz, nz), (vsx, nx))):
             wait(hs.at[0, k, p], buf.at[p, 0, 0, pl.ds(0, n - 1)])
@@ -381,8 +414,8 @@
             pltpu.VMEM((n, NB, 3 * NB), BF16),
         ]
     scratch += [
-        dma((5,)), dma((1,)), dma((npan,)), dma((npan,)), dma((3, npan)), dma((3, npan)),
-        dma((2, 2, npan)), dma((2, 2, npan)),
+        dma((5,)), dma((1,)), dma((3, npan, ny - 1)), dma((3, npan, ny - 1)), dma((3, npan)), dma((3, npan)),
+        dma((1, 2, npan)), dma((1, 2, npan)),
         dma((npan, nc)), dma((npan, nc)), dma((npan, nc)), dma((npan, nc)), dma((npan, nc)), dma((npan, nc)),
         dma,
     ]
@@ -393,7 +426,7 @@
         out_specs=any_space,
         scratch_shapes=scratch,
         compiler_params=pltpu.CompilerParams(
-            collective_id=0, has_side_effects=True, vmem_limit_bytes=48 * 1024 * 1024
+            collective_id=0, has_side_effects=True, vmem_limit_bytes=67_043_328
         ),
     )(
         window, leaf_vecs, leaf_t,

time: 108 us -> 114 us (1.056)
  the two profiles are of different devices: /device:TPU:16 before, /device:TPU:24 now
where the time goes in v2:
time: 114 us
  Pallas kernels  110 us (96%)
  local copies, waits for them, and re-layouts  3.16 us (3%)
    pallas_call x1, Pallas kernels, local(): pl.pallas_call(functools.partial(kernel, (nx, nz, ny, nc, mr, ncl, npan))...  110 us
    unnamed x1, local copies, waits for them, and re-layouts  3.16 us

profile of v2, /device:TPU:24, one launch (start us, length us, event | category | flops | bytes accessed | tf_op | source)
XLA Modules:
  0.0 113.5 jit_solution(16291243826276846146)
XLA Ops:
  0.0 110.4 %shard_map.55 = f32[512,1024]{1,0:T(8,128)} custom-call(f32[512,1024]{1,0:T(8,128)} %refs_0_.1, f32[2,32,128]{2,1,0:T(8,128)} %refs_1_.1, f32[2,128,128]{2,1,0:T(8,128)} %refs_2_.1, f32[2,16,8,128]{3,2,1,0:T(8,128)} %bitcast.2, f32[2,16,8,128]{3,2,1,0:T(8,128)} %bitcast.3), custom_call_target="tpu_custom_call" | custom-call | tf_op jit(solution)/shard_map/pallas_call | solution.py:422
  110.4 3.2 %copy.7 = f32[512,1024]{1,0:T(8,128)} copy(f32[512,1024]{1,0:T(8,128)} %shard_map.55) | data formatting | bytes 4194304

commit v3 on v1

--- a/solution.py
+++ b/solution.py
@@ -12,7 +12,7 @@
 NB = 128
 NX = 4
 CORES = 2
-CHUNKS = 2
+CHUNKS = 4
 
 
 def split(value):
@@ -393,7 +393,7 @@
         out_specs=any_space,
         scratch_shapes=scratch,
         compiler_params=pltpu.CompilerParams(
-            collective_id=0, has_side_effects=True, vmem_limit_bytes=48 * 1024 * 1024
+            collective_id=0, has_side_effects=True, vmem_limit_bytes=67_043_328
         ),
     )(
         window, leaf_vecs, leaf_t,

time: 108 us -> 102 us (0.944)
  the two profiles are of different devices: /device:TPU:16 before, /device:TPU:8 now
where the time goes in v3:
time: 102 us
  Pallas kernels  99.1 us (97%)
  local copies, waits for them, and re-layouts  3.16 us (3%)
    pallas_call x1, Pallas kernels, local(): pl.pallas_call(functools.partial(kernel, (nx, nz, ny, nc, mr, ncl, npan))...  99.1 us
    unnamed x1, local copies, waits for them, and re-layouts  3.16 us

profile of v3, /device:TPU:8, one launch (start us, length us, event | category | flops | bytes accessed | tf_op | source)
XLA Modules:
  0.0 102.3 jit_solution(12165724495733070185)
XLA Ops:
  0.0 99.1 %shard_map.55 = f32[512,1024]{1,0:T(8,128)} custom-call(f32[512,1024]{1,0:T(8,128)} %refs_0_.1, f32[2,32,128]{2,1,0:T(8,128)} %refs_1_.1, f32[2,128,128]{2,1,0:T(8,128)} %refs_2_.1, f32[2,16,8,128]{3,2,1,0:T(8,128)} %bitcast.2, f32[2,16,8,128]{3,2,1,0:T(8,128)} %bitcast.3), custom_call_target="tpu_custom_call" | custom-call | tf_op jit(solution)/shard_map/pallas_call | solution.py:389
  99.1 3.2 %copy.7 = f32[512,1024]{1,0:T(8,128)} copy(f32[512,1024]{1,0:T(8,128)} %shard_map.55) | data formatting | bytes 4194304
